TPU v7x, 32 devices: a whole 2x2x4 slice. The times are simulated.
32 devices in a mesh: tensor: 4 (over z), dp: 4 (over y, x), replica: 2 (over core).
Axes of the slice: x: 2, y: 2, z: 4, core: 2. Of those that a mesh axis runs over, the one named last changes fastest.
Arguments:
- states: bfloat16 [8, 256, 4096], P(('dp', 'replica')), may hold values from -6 to 6
- norm_gain: float32 [4096], replicated, may hold values from 0.26 to 4.4
- gate_up: bfloat16 [4096, 2, 14336], P('replica', None, 'tensor'), may hold values from -0.09375 to 0.09375
- cotangent: bfloat16 [8, 256, 14336], P(('dp', 'replica'), None, 'tensor'), may hold values from -120 to 120
- prompt: bfloat16 [32, 4096], replicated, may hold values from -6 to 6
- step_sizes: float32 [3], replicated, may hold values from 0.3 to 1
- insert_at: int32 [8], P(('dp', 'replica')), may hold values from 0 to 224, as said below
- lengths: int32 [8], P(('dp', 'replica')), may hold values from 128 to 256, as said below
Outputs:
- prompt_final: float32 [32, 4096], P(None, 'tensor')
- weight_step: bfloat16 [4096, 2, 14336], P(('dp', 'replica'), None, 'tensor')
Inputs may be any that keep to these rules, and one draw needn't show every extreme that they name: Each prompt lies inside its sequence: insert_at[b] + 32 <= lengths[b]; in every draw some prompt begins at row 0 and some prompt ends at the last row 255. `lengths`: in every draw some sequence has all 256 rows live and some has 128.
All inputs are finite; a program needn't handle non-finite values.
Results may differ from a plain program's by a relative error of at most 0.012.
Values may be sent and summed in bfloat16 or wider, within the bound.
A program may use at most 320 MiB of HBM per device.

v0:
```python
import jax
import jax.numpy as jnp
from jax import lax
from jax.sharding import PartitionSpec as P

D = 4096
FF = 14336


def row_scale(feature_rows):
    return lax.rsqrt(jnp.mean(feature_rows * feature_rows, axis=-1, keepdims=True) + 1e-05)


def silu_parts(gate_values):
    sigmoid_value = jax.nn.sigmoid(gate_values)
    return (
        gate_values * sigmoid_value,
        sigmoid_value * (1.0 + gate_values * (1.0 - sigmoid_value)),
    )


def hidden_grads(normalized, weight_pair, cotan_rows):
    unit_count = weight_pair.shape[1] // 2
    projected = jnp.dot(normalized, weight_pair, preferred_element_type=jnp.float32)
    activated, derivative = silu_parts(projected[:, :unit_count])
    up_part = projected[:, unit_count:]
    return jnp.concatenate(
        [cotan_rows * up_part * derivative, cotan_rows * activated], axis=1
    ).astype(jnp.bfloat16)


def norm_back(shifted, inverse_rms, norm_gain, feature_grad):
    feature_mean = jnp.mean(shifted * norm_gain * feature_grad, axis=-1, keepdims=True)
    return (
        inverse_rms * norm_gain * feature_grad
        - shifted * (inverse_rms * inverse_rms * inverse_rms) * feature_mean
    )


def per_device(states, norm_gain, gate_up, cotangent, prompt, step_sizes, insert_at, lengths):
    gathered = lax.all_gather(gate_up, "replica", axis=0, tiled=True)
    feature_count = gathered.shape[0]
    unit_count = gathered.shape[2]
    weight_pair = gathered.reshape(feature_count, 2 * unit_count)
    seq_states = states[0]
    seq_cotan = cotangent[0].astype(jnp.float32)
    prompt_start = insert_at[0]
    seq_length = lengths[0]
    prompt_count = prompt.shape[0]
    prompt_base = lax.dynamic_slice_in_dim(seq_states, prompt_start, prompt_count, 0).astype(
        jnp.float32
    )
    prompt_cotan = lax.dynamic_slice_in_dim(seq_cotan, prompt_start, prompt_count, 0)
    adversary = prompt.astype(jnp.float32)
    for attack_step in range(step_sizes.shape[0]):
        shifted = prompt_base + adversary
        inverse_rms = row_scale(shifted)
        normalized = (shifted * inverse_rms * norm_gain).astype(jnp.bfloat16)
        unit_grads = hidden_grads(normalized, weight_pair, prompt_cotan)
        feature_grad = lax.dot_general(
            unit_grads, weight_pair, (((1,), (1,)), ((), ())), preferred_element_type=jnp.float32
        )
        feature_grad = lax.psum(feature_grad, "tensor")
        summed_grad = lax.psum(
            norm_back(shifted, inverse_rms, norm_gain, feature_grad), ("dp", "replica")
        )
        adversary = adversary + step_sizes[attack_step] * summed_grad * lax.rsqrt(
            jnp.mean(summed_grad * summed_grad, axis=-1, keepdims=True) + 1e-06
        )
    full_rows = lax.dynamic_update_slice_in_dim(
        seq_states.astype(jnp.float32), prompt_base + adversary, prompt_start, 0
    )
    full_normed = (full_rows * row_scale(full_rows) * norm_gain).astype(jnp.bfloat16)
    positions = lax.broadcasted_iota(jnp.int32, (full_rows.shape[0], 1), 0)
    live_cotan = jnp.where(positions < seq_length, seq_cotan, 0.0)
    token_grads = hidden_grads(full_normed, weight_pair, live_cotan)
    received = lax.all_to_all(
        full_normed, ("dp", "replica"), split_axis=1, concat_axis=0, tiled=True
    )
    weight_grad = lax.dot_general(
        received,
        lax.all_gather(token_grads, ("dp", "replica"), axis=0, tiled=True),
        (((0,), (0,)), ((), ())),
        preferred_element_type=jnp.float32,
    )
    squares = lax.psum(jnp.sum(weight_grad * weight_grad), ("tensor", "dp", "replica"))
    weight_step = (weight_grad * lax.rsqrt(squares / (2 * D * FF) + 1e-06)).astype(jnp.bfloat16)
    weight_step = weight_step.reshape(weight_grad.shape[0], 2, unit_count)
    column_count = adversary.shape[1] // lax.axis_size("tensor")
    prompt_final = lax.dynamic_slice_in_dim(
        adversary, lax.axis_index("tensor") * column_count, column_count, 1
    )
    return (prompt_final, weight_step)


def solution(mesh):
    return jax.shard_map(
        per_device,
        mesh=mesh,
        in_specs=(
            P(("dp", "replica"), None, None),
            P(),
            P("replica", None, "tensor"),
            P(("dp", "replica"), None, "tensor"),
            P(),
            P(),
            P(("dp", "replica")),
            P(("dp", "replica")),
        ),
        out_specs=(P(None, "tensor"), P(("dp", "replica"), None, "tensor")),
        check_vma=False,
    )
```

profile of v0, /device:TPU:0, one launch (start us, length us, event | category | flops | bytes accessed | tf_op | source)
XLA Modules:
  0.0 889.3 jit_solution(5123396470353676943)
XLA Ops:
  8.8 3.8 convert_element_type.43
  12.8 83.6 %all-gather.3.cloned.1.call-done = bf16[4096,2,3584]{2,1,0:T(2,128)(2,1)} async-done(((bf16[2048,2,3584]{2,1,0:T(2,128)(2,1)}), bf16[4096,2,3584]{2,1,0:T(2,128)(2,1)}) %all-gather.3.cloned.1.call-update) | async-done | bytes 58720272 | tf_op jit(solution)/shard_map/all_gather | solution.py:41
  96.4 39.3 %copy.16 = bf16[512,8,2,3584]{3,1,2,0:T(8,128)(2,1)} copy(bf16[512,8,2,3584]{3,2,1,0:T(2,128)(2,1)} %bitcast.75) | data formatting | bytes 117440512
  135.7 21.5 %fusion.23 = f32[32,7168]{1,0:T(8,128)S(1)} fusion(bf16[4096,7168]{1,0:T(8,128)(2,1)} %bitcast.68, bf16[32,4096]{1,0:T(8,128)(2,1)S(1)} %copy-done.2, f32[4096]{0:T(1024)S(1)} %copy-done.5, f32[32]{0:T(128)S(1)} %get-tuple-element.24, bf16[1,256,4096]{2,1,0:T(8,128)(2,1)S(1)} %copy-done.1, s32[]{:T(128)S(6)} %select_n.12), kind=kOutput, calls=%fused_computation.64 | convolution fusion | flops 1879834624 | bytes 60178948 | tf_op jit(solution)/shard_map/dot_general | solution.py:24
  158.5 24.7 %fusion.8 = f32[32,4096]{1,0:T(8,128)} fusion(bf16[4096,7168]{1,0:T(8,128)(2,1)} %bitcast.69, bf16[32,3584]{1,0:T(8,128)(2,1)S(1)} %get-tuple-element.15, bf16[32,3584]{1,0:T(8,128)(2,1)S(1)} %get-tuple-element.14), kind=kOutput, calls=%fused_computation.43 | convolution fusion | flops 1879965696 | bytes 59703296 | tf_op jit(solution)/shard_map/dot_general | solution.py:60
  183.3 39.6 %all-reduce.7.cloned.1.call-done = f32[32,4096]{1,0:T(8,128)} async-done(((f32[32,4096]{1,0:T(8,128)}), f32[32,4096]{1,0:T(8,128)}) %all-reduce.7.cloned.1.call-update) | async-done | bytes 524304 | tf_op jit(solution)/shard_map/psum | solution.py:63
  226.9 54.0 %all-reduce.9.cloned.1.call-done = f32[32,4096]{1,0:T(8,128)} async-done(((f32[32,4096]{1,0:T(8,128)}), f32[32,4096]{1,0:T(8,128)}) %all-reduce.9.cloned.1.call-update) | async-done | bytes 524304 | tf_op jit(solution)/shard_map/psum | solution.py:64
  284.0 21.5 %fusion.24 = f32[32,7168]{1,0:T(8,128)S(1)} fusion(bf16[4096,7168]{1,0:T(8,128)(2,1)} %bitcast.70, f32[32,4096]{1,0:T(8,128)S(1)} %get-tuple-element.7, f32[32]{0:T(128)S(1)} %get-tuple-element.22, f32[4096]{0:T(1024)S(1)} %copy-done.5), kind=kOutput, calls=%fused_computation.65 | convolution fusion | flops 1879441408 | bytes 60178560 | tf_op jit(solution)/shard_map/dot_general | solution.py:24
  306.9 24.7 %fusion.12 = f32[32,4096]{1,0:T(8,128)} fusion(bf16[4096,7168]{1,0:T(8,128)(2,1)} %bitcast.71, bf16[32,3584]{1,0:T(8,128)(2,1)S(1)} %get-tuple-element.13, bf16[32,3584]{1,0:T(8,128)(2,1)S(1)} %get-tuple-element.12), kind=kOutput, calls=%fused_computation.47 | convolution fusion | flops 1879965696 | bytes 59703296 | tf_op jit(solution)/shard_map/dot_general | solution.py:60
  331.6 37.7 %all-reduce.11.cloned.1.call-done = f32[32,4096]{1,0:T(8,128)} async-done(((f32[32,4096]{1,0:T(8,128)}), f32[32,4096]{1,0:T(8,128)}) %all-reduce.11.cloned.1.call-update) | async-done | bytes 524304 | tf_op jit(solution)/shard_map/psum | solution.py:63
  372.9 54.4 %all-reduce.13.cloned.1.call-done = f32[32,4096]{1,0:T(8,128)} async-done(((f32[32,4096]{1,0:T(8,128)}), f32[32,4096]{1,0:T(8,128)}) %all-reduce.13.cloned.1.call-update) | async-done | bytes 524304 | tf_op jit(solution)/shard_map/psum | solution.py:64
  428.5 2.6 multiply_reduce_fusion.4
  431.1 21.4 %fusion.25 = f32[32,7168]{1,0:T(8,128)S(1)} fusion(bf16[4096,7168]{1,0:T(8,128)(2,1)} %bitcast.72, f32[32]{0:T(128)S(1)} %get-tuple-element.20, f32[4096]{0:T(1024)S(1)} %copy-done.5, f32[32,4096]{1,0:T(8,128)S(1)} %get-tuple-element.5, bf16[1,256,4096]{2,1,0:T(8,128)(2,1)S(1)} %copy-done.1, s32[]{:T(128)S(6)} %select_n.12), kind=kOutput, calls=%fused_computation.66 | convolution fusion | flops 1879703552 | bytes 60441092 | tf_op jit(solution)/shard_map/dot_general | solution.py:24
  453.8 24.7 %fusion.16 = f32[32,4096]{1,0:T(8,128)} fusion(bf16[4096,7168]{1,0:T(8,128)(2,1)} %bitcast.73, bf16[32,3584]{1,0:T(8,128)(2,1)S(1)} %get-tuple-element.11, bf16[32,3584]{1,0:T(8,128)(2,1)S(1)} %get-tuple-element.10), kind=kOutput, calls=%fused_computation.51 | convolution fusion | flops 1879965696 | bytes 59703296 | tf_op jit(solution)/shard_map/dot_general | solution.py:60
  478.6 2.5 copy.13
  481.1 35.2 %all-reduce.15.cloned.1.call-done = f32[32,4096]{1,0:T(8,128)} async-done(((f32[32,4096]{1,0:T(8,128)}), f32[32,4096]{1,0:T(8,128)}) %all-reduce.15.cloned.1.call-update) | async-done | bytes 524304 | tf_op jit(solution)/shard_map/psum | solution.py:63
  520.2 3.9 bitcast_convert_fusion
  524.8 49.5 %all-reduce.17.cloned.1.call-done = f32[32,4096]{1,0:T(8,128)} async-done(((f32[32,4096]{1,0:T(8,128)}), f32[32,4096]{1,0:T(8,128)}) %all-reduce.17.cloned.1.call-update) | async-done | bytes 524304 | tf_op jit(solution)/shard_map/psum | solution.py:64
  575.5 2.7 convert_add_fusion
  578.8 11.9 %dynamic_update_slice.3 = f32[256,4096]{0,1:T(8,128)} dynamic-update-slice(f32[256,4096]{0,1:T(8,128)} %bitcast_convert_fusion, f32[32,4096]{0,1:T(8,128)S(1)} %copy.14, s32[]{:T(128)S(6)} %select_n.12, s32[]{:T(128)} %constant.15.clone.1) | dynamic-update-slice | bytes 1048580 | tf_op jit(solution)/shard_map/dynamic_update_slice | solution.py:70
  590.7 2.9 multiply_reduce_fusion.1
  595.9 28.3 %fusion.39 = f32[256,7168]{1,0:T(8,128)} fusion(bf16[256,4096]{0,1:T(8,128)(2,1)} %multiply_convert_fusion.1, bf16[4096,7168]{1,0:T(8,128)(2,1)} %bitcast.74), kind=kOutput, calls=%fused_computation.95 | convolution fusion | flops 15032385536 | bytes 68157440 | tf_op jit(solution)/shard_map/dot_general | solution.py:24
  624.2 4.1 fusion.1
  628.3 2.3 pad_maximum_fusion
  630.6 3.8 all-to-all-start
  636.0 41.6 %all-to-all-done = bf16[256,8,512]{0,2,1:T(8,128)(2,1)S(1)} async-done(((bf16[256,8,512]{0,2,1:T(8,128)(2,1)}), bf16[256,8,512]{0,2,1:T(8,128)(2,1)S(1)}, u32[]{:S(2)}, u32[]{:S(2)}) %all-to-all-start) | async-done | bytes 2097184 | tf_op jit(solution)/shard_map/all_to_all | solution.py:77
  677.6 2.4 copy.15
  680.0 109.1 %all-gather.5.cloned.1.call-done = bf16[2048,7168]{1,0:T(8,128)(2,1)} async-done(((bf16[256,7168]{1,0:T(8,128)(2,1)}), bf16[2048,7168]{1,0:T(8,128)(2,1)}) %all-gather.5.cloned.1.call-update) | async-done | bytes 29360144 | tf_op jit(solution)/shard_map/all_gather | solution.py:82
  789.1 26.1 %multiply_reduce_fusion = (f32[]{:T(128)}, f32[512,7168]{1,0:T(8,128)}) fusion(bf16[2048,512]{1,0:T(8,128)(2,1)} %bitcast.77, bf16[2048,7168]{1,0:T(8,128)(2,1)} %all-gather.5.cloned.1.call-done), kind=kOutput, calls=%fused_computation.1 | convolution fusion | flops 15039725568 | bytes 46137348 | tf_op jit(solution)/shard_map/dot_general | solution.py:80
  815.2 39.7 %psum.55 = f32[]{:T(128)} all-reduce(f32[]{:T(128)} %get-tuple-element.25), channel_id=1, replica_groups=mesh['tensor'=4,'dp'=4,'replica'=2] {'tensor','dp','replica'}, use_global_device_ids=true, to_apply=%region_17.18 | all-reduce | flops 1 | bytes 8 | tf_op jit(solution)/shard_map/psum | solution.py:86
  855.6 9.8 %multiply_convert_fusion = bf16[512,7168]{1,0:T(8,128)(2,1)} fusion(f32[512,7168]{1,0:T(8,128)} %get-tuple-element.26, f32[]{:T(128)S(6)} %rsqrt.75), kind=kLoop, calls=%fused_computation | loop fusion | flops 7340032 | bytes 22020100 | tf_op jit(solution)/shard_map/convert_element_type | solution.py:87
  865.4 16.9 %reshape.113 = bf16[512,2,3584]{2,1,0:T(2,128)(2,1)} reshape(bf16[512,7168]{1,0:T(8,128)(2,1)} %multiply_convert_fusion) | data formatting | bytes 14680064 | tf_op jit(solution)/shard_map/reshape | solution.py:88
  (59 shorter events, 26.6 us)
Async XLA Ops:
  7.2 89.3 %all-gather.3.cloned.1.call-start = ((), (), s32[]{:S(2)}) async-start(), calls=%async_computation.1 | async-start | bytes 88080384 | tf_op jit(solution)/shard_map/all_gather | solution.py:41
  7.9 4.6 copy-start.1
  7.9 4.6 copy-start.2
  7.9 214.9 %all-reduce.7.cloned.1.call-start = ((), (), s32[]{:S(2)}) async-start(), calls=%async_computation.2 | async-start | bytes 1048576 | tf_op jit(solution)/shard_map/psum | solution.py:63
  96.4 39.3 %copy-start.5 = (f32[4096]{0:T(1024)S(1)}, f32[4096]{0:T(1024)}, u32[]{:S(2)}) copy-start(f32[4096]{0:T(1024)} %param.9) | copy-start | bytes 49156
  183.2 43.0 %copy-start.6 = (f32[3]{0:T(128)S(1)}, f32[3]{0:T(128)}, u32[]{:S(2)}) copy-start(f32[3]{0:T(128)} %param.13) | copy-start | bytes 40
  183.3 97.6 %all-reduce.9.cloned.1.call-start = ((), (), s32[]{:S(2)}) async-start(), calls=%async_computation.3 | async-start | bytes 1048576 | tf_op jit(solution)/shard_map/psum | solution.py:64
  226.2 143.1 %all-reduce.11.cloned.1.call-start = ((), (), s32[]{:S(2)}) async-start(), calls=%async_computation.4 | async-start | bytes 1048576 | tf_op jit(solution)/shard_map/psum | solution.py:63
  331.5 96.9 %copy-start.4 = (f32[32,4096]{1,0:T(8,128)S(1)}, f32[32,4096]{1,0:T(8,128)}, u32[]{:S(2)}) copy-start(f32[32,4096]{1,0:T(8,128)} %all-reduce.9.cloned.1.call-done) | copy-start | bytes 1572868
  331.6 95.7 %all-reduce.13.cloned.1.call-start = ((), (), s32[]{:S(2)}) async-start(), calls=%async_computation.5 | async-start | bytes 1048576 | tf_op jit(solution)/shard_map/psum | solution.py:64
  372.6 143.8 %all-reduce.15.cloned.1.call-start = ((), (), s32[]{:S(2)}) async-start(), calls=%async_computation.6 | async-start | bytes 1048576 | tf_op jit(solution)/shard_map/psum | solution.py:63
  478.6 95.8 %all-reduce.17.cloned.1.call-start = ((), (), s32[]{:S(2)}) async-start(), calls=%async_computation.7 | async-start | bytes 1048576 | tf_op jit(solution)/shard_map/psum | solution.py:64
  519.6 269.4 %all-gather.5.cloned.1.call-start = ((), (), s32[]{:S(2)}) async-start(), calls=%async_computation.8 | async-start | bytes 33030144 | tf_op jit(solution)/shard_map/all_gather | solution.py:82
  590.7 3.4 copy-start
  595.9 28.3 %copy-start.3 = (bf16[1,256,3584]{2,1,0:T(8,128)(2,1)S(1)}, bf16[1,256,3584]{2,1,0:T(8,128)(2,1)}, u32[]{:S(2)}) copy-start(bf16[1,256,3584]{2,1,0:T(8,128)(2,1)} %param.11) | copy-start | bytes 5505028
  630.6 47.0 %all-to-all-start = ((bf16[256,8,512]{0,2,1:T(8,128)(2,1)}), bf16[256,8,512]{0,2,1:T(8,128)(2,1)S(1)}, u32[]{:S(2)}, u32[]{:S(2)}) async-start(bf16[256,8,512]{0,2,1:T(8,128)(2,1)} %bitcast.8), calls=%async_computation | async-start | bytes 4194304 | tf_op jit(solution)/shard_map/all_to_all | solution.py:77
Sparse Core Ops, SparseCore 0:
  9.5 86.8 all-gather.2
  183.4 39.4 all-reduce.6
  226.3 54.5 all-reduce.8
  331.7 37.5 all-reduce.10
  372.7 54.5 all-reduce.12
  478.7 37.5 all-reduce.14
  519.8 54.5 all-reduce.16
  630.7 158.2 all-gather.4
where the time goes:
time: 900 us; the launch traced here: 889 us
  waiting for transfers between devices  505 us (56%)
  matrix products  193 us (21%)
  local copies, waits for them, and re-layouts  76.3 us (8%)
  other arithmetic  53.3 us (6%)
  blocking collectives  39.7 us (4%)
  between operations  16.6 us (2%)
    psum x3, waiting for transfers between devices, per_device(): lax.psum(norm_back(shifted, inverse_rms, norm_gain, feature_grad), ('dp',...  158 us
    psum x3, waiting for transfers between devices, per_device(): feature_grad = lax.psum(feature_grad, 'tensor')  112 us
    all_gather x1, waiting for transfers between devices, per_device(): lax.all_gather(token_grads, ('dp', 'replica'), axis=0, tiled=True)  109 us
    dot_general x4, matrix products, hidden_grads(): jnp.dot(normalized, weight_pair, preferred_element_type=jnp.float32)  92.8 us
    all_gather x1, waiting for transfers between devices, per_device(): gathered = lax.all_gather(gate_up, 'replica', axis=0, tiled=True)  83.6 us
    dot_general x3, matrix products, per_device(): lax.dot_general(unit_grads, weight_pair, (((1,), (1,)), ((), ())), prefer...  74.1 us
    unnamed x16, local copies, waits for them, and re-layouts  42.3 us
    all_to_all x1, waiting for transfers between devices, per_device(): lax.all_to_all(full_normed, ('dp', 'replica'), split_axis=1, concat_axis=...  41.6 us
  transfers between devices with their start and end apart: 9, of which 9 were waited for; matrix products, arithmetic and copies ran while one was open for 2% of the time, Pallas kernels for 0%

commit v1 on v0

--- a/solution.py
+++ b/solution.py
@@ -74,9 +74,19 @@
     positions = lax.broadcasted_iota(jnp.int32, (full_rows.shape[0], 1), 0)
     live_cotan = jnp.where(positions < seq_length, seq_cotan, 0.0)
     token_grads = hidden_grads(full_normed, weight_pair, live_cotan)
-    received = lax.all_to_all(
-        full_normed, ("dp", "replica"), split_axis=1, concat_axis=0, tiled=True
-    )
+    ways, here = (lax.axis_size(("dp", "replica")), lax.axis_index(("dp", "replica")))
+    width = full_normed.shape[1] // ways
+    dims = list(full_normed.shape)
+    dims[1] = width
+    height = dims[0]
+    dims[0] = height * ways
+    full = jnp.zeros(dims, full_normed.dtype)
+    for mask in range(ways):
+        part = lax.dynamic_slice_in_dim(full_normed, (here ^ mask) * width, width, axis=1)
+        if mask:
+            part = lax.ppermute(part, ("dp", "replica"), [(d, d ^ mask) for d in range(ways)])
+        full = lax.dynamic_update_slice_in_dim(full, part, (here ^ mask) * height, axis=0)
+    received = full
     weight_grad = lax.dot_general(
         received,
         lax.all_gather(token_grads, ("dp", "replica"), axis=0, tiled=True),

time: 900 us -> 886 us (0.984)
    all_to_all x1 -> x0, waiting for transfers between devices: 41.6 us -> none  [per_device(): lax.all_to_all(full_normed, ('dp', 'replica'), split_axis=1, concat_axis=...]
    ppermute x0 -> x7, waiting for transfers between devices: none -> 30 us  [per_device(): lax.ppermute(part, ('dp', 'replica'), [(d, d ^ mask) for d in range(ways)])]
    dynamic_update_slice x1, local copies, waits for them, and re-layouts: 11.9 us -> 2.91 us  [per_device(): lax.dynamic_update_slice_in_dim(seq_states.astype(jnp.float32), prompt_ba...]
    unnamed x16 -> x15, local copies, waits for them, and re-layouts: 42.3 us -> 41.3 us
  transfers between devices with their start and end apart: 9 -> 15, of which waited for: 9 -> 13; matrix products, arithmetic and copies ran while one was open for 2% -> 2% of each run, Pallas kernels for 0% -> 0%
where the time goes in v1:
time: 886 us; the launch traced here: 876 us
  waiting for transfers between devices  504 us (57%)
  matrix products  191 us (22%)
  local copies, waits for them, and re-layouts  69.5 us (8%)
  other arithmetic  51 us (6%)
  blocking collectives  39.7 us (4%)
  between operations  16.7 us (2%)
    psum x3, waiting for transfers between devices, per_device(): lax.psum(norm_back(shifted, inverse_rms, norm_gain, feature_grad), ('dp',...  160 us
    psum x3, waiting for transfers between devices, per_device(): feature_grad = lax.psum(feature_grad, 'tensor')  115 us
    all_gather x1, waiting for transfers between devices, per_device(): lax.all_gather(token_grads, ('dp', 'replica'), axis=0, tiled=True)  115 us
    dot_general x4, matrix products, hidden_grads(): jnp.dot(normalized, weight_pair, preferred_element_type=jnp.float32)  90.3 us
    all_gather x1, waiting for transfers between devices, per_device(): gathered = lax.all_gather(gate_up, 'replica', axis=0, tiled=True)  83.6 us
    dot_general x3, matrix products, per_device(): lax.dot_general(unit_grads, weight_pair, (((1,), (1,)), ((), ())), prefer...  74.1 us
    unnamed x15, local copies, waits for them, and re-layouts  41.3 us
    psum x1, blocking collectives, per_device(): lax.psum(jnp.sum(weight_grad * weight_grad), ('tensor', 'dp', 'replica'))  39.7 us
  transfers between devices with their start and end apart: 15, of which 13 were waited for; matrix products, arithmetic and copies ran while one was open for 2% of the time, Pallas kernels for 0%

profile of v1, /device:TPU:0, one launch (start us, length us, event | category | flops | bytes accessed | tf_op | source)
XLA Modules:
  0.0 876.4 jit_solution(4359876409488670402)
XLA Ops:
  8.8 3.8 convert_element_type.43
  12.8 83.6 %all-gather.3.cloned.1.call-done = bf16[4096,2,3584]{2,1,0:T(2,128)(2,1)} async-done(((bf16[2048,2,3584]{2,1,0:T(2,128)(2,1)}), bf16[4096,2,3584]{2,1,0:T(2,128)(2,1)}) %all-gather.3.cloned.1.call-update) | async-done | bytes 58720272 | tf_op jit(solution)/shard_map/all_gather | solution.py:41
  96.4 39.3 %copy.10 = bf16[512,8,2,3584]{3,1,2,0:T(8,128)(2,1)} copy(bf16[512,8,2,3584]{3,2,1,0:T(2,128)(2,1)} %bitcast.72) | data formatting | bytes 117440512
  135.7 21.5 %fusion.23 = f32[32,7168]{1,0:T(8,128)S(1)} fusion(bf16[4096,7168]{1,0:T(8,128)(2,1)} %bitcast.65, bf16[32,4096]{1,0:T(8,128)(2,1)S(1)} %copy-done.2, f32[4096]{0:T(1024)S(1)} %copy-done.4, f32[32]{0:T(128)S(1)} %get-tuple-element.32, bf16[1,256,4096]{2,1,0:T(8,128)(2,1)S(1)} %copy-done.1, s32[]{:T(128)S(6)} %select_n.60), kind=kOutput, calls=%fused_computation.64 | convolution fusion | flops 1879834624 | bytes 60178948 | tf_op jit(solution)/shard_map/dot_general | solution.py:24
  158.5 24.7 %fusion.8 = f32[32,4096]{1,0:T(8,128)} fusion(bf16[4096,7168]{1,0:T(8,128)(2,1)} %bitcast.66, bf16[32,3584]{1,0:T(8,128)(2,1)S(1)} %get-tuple-element.15, bf16[32,3584]{1,0:T(8,128)(2,1)S(1)} %get-tuple-element.14), kind=kOutput, calls=%fused_computation.43 | convolution fusion | flops 1879965696 | bytes 59703296 | tf_op jit(solution)/shard_map/dot_general | solution.py:60
  183.3 39.6 %all-reduce.7.cloned.1.call-done = f32[32,4096]{1,0:T(8,128)} async-done(((f32[32,4096]{1,0:T(8,128)}), f32[32,4096]{1,0:T(8,128)}) %all-reduce.7.cloned.1.call-update) | async-done | bytes 524304 | tf_op jit(solution)/shard_map/psum | solution.py:63
  226.9 54.0 %all-reduce.9.cloned.1.call-done = f32[32,4096]{1,0:T(8,128)} async-done(((f32[32,4096]{1,0:T(8,128)}), f32[32,4096]{1,0:T(8,128)}) %all-reduce.9.cloned.1.call-update) | async-done | bytes 524304 | tf_op jit(solution)/shard_map/psum | solution.py:64
  284.0 21.5 %fusion.24 = f32[32,7168]{1,0:T(8,128)S(1)} fusion(bf16[4096,7168]{1,0:T(8,128)(2,1)} %bitcast.67, f32[32,4096]{1,0:T(8,128)S(1)} %get-tuple-element.7, f32[32]{0:T(128)S(1)} %get-tuple-element.30, f32[4096]{0:T(1024)S(1)} %copy-done.4), kind=kOutput, calls=%fused_computation.65 | convolution fusion | flops 1879441408 | bytes 60178560 | tf_op jit(solution)/shard_map/dot_general | solution.py:24
  306.9 24.7 %fusion.12 = f32[32,4096]{1,0:T(8,128)} fusion(bf16[4096,7168]{1,0:T(8,128)(2,1)} %bitcast.68, bf16[32,3584]{1,0:T(8,128)(2,1)S(1)} %get-tuple-element.13, bf16[32,3584]{1,0:T(8,128)(2,1)S(1)} %get-tuple-element.12), kind=kOutput, calls=%fused_computation.47 | convolution fusion | flops 1879965696 | bytes 59703296 | tf_op jit(solution)/shard_map/dot_general | solution.py:60
  331.6 37.7 %all-reduce.11.cloned.1.call-done = f32[32,4096]{1,0:T(8,128)} async-done(((f32[32,4096]{1,0:T(8,128)}), f32[32,4096]{1,0:T(8,128)}) %all-reduce.11.cloned.1.call-update) | async-done | bytes 524304 | tf_op jit(solution)/shard_map/psum | solution.py:63
  373.1 54.2 %all-reduce.13.cloned.1.call-done = f32[32,4096]{1,0:T(8,128)} async-done(((f32[32,4096]{1,0:T(8,128)}), f32[32,4096]{1,0:T(8,128)}) %all-reduce.13.cloned.1.call-update) | async-done | bytes 524304 | tf_op jit(solution)/shard_map/psum | solution.py:64
  428.5 2.6 multiply_reduce_fusion.4
  431.1 21.4 %fusion.25 = f32[32,7168]{1,0:T(8,128)S(1)} fusion(bf16[4096,7168]{1,0:T(8,128)(2,1)} %bitcast.69, f32[32]{0:T(128)S(1)} %get-tuple-element.28, f32[4096]{0:T(1024)S(1)} %copy-done.4, f32[32,4096]{1,0:T(8,128)S(1)} %get-tuple-element.5, bf16[1,256,4096]{2,1,0:T(8,128)(2,1)S(1)} %copy-done.1, s32[]{:T(128)S(6)} %select_n.60), kind=kOutput, calls=%fused_computation.66 | convolution fusion | flops 1879703552 | bytes 60441092 | tf_op jit(solution)/shard_map/dot_general | solution.py:24
  453.8 24.7 %fusion.16 = f32[32,4096]{1,0:T(8,128)} fusion(bf16[4096,7168]{1,0:T(8,128)(2,1)} %bitcast.70, bf16[32,3584]{1,0:T(8,128)(2,1)S(1)} %get-tuple-element.11, bf16[32,3584]{1,0:T(8,128)(2,1)S(1)} %get-tuple-element.10), kind=kOutput, calls=%fused_computation.51 | convolution fusion | flops 1879965696 | bytes 59703296 | tf_op jit(solution)/shard_map/dot_general | solution.py:60
  478.6 37.7 %all-reduce.15.cloned.1.call-done = f32[32,4096]{1,0:T(8,128)} async-done(((f32[32,4096]{1,0:T(8,128)}), f32[32,4096]{1,0:T(8,128)}) %all-reduce.15.cloned.1.call-update) | async-done | bytes 524304 | tf_op jit(solution)/shard_map/psum | solution.py:63
  519.7 2.5 bitcast_convert_fusion
  522.9 51.5 %all-reduce.17.cloned.1.call-done = f32[32,4096]{1,0:T(8,128)} async-done(((f32[32,4096]{1,0:T(8,128)}), f32[32,4096]{1,0:T(8,128)}) %all-reduce.17.cloned.1.call-update) | async-done | bytes 524304 | tf_op jit(solution)/shard_map/psum | solution.py:64
  575.5 2.7 convert_add_fusion
  578.2 2.9 dynamic_update_slice.27
  581.1 2.7 multiply_reduce_fusion.1
  585.1 25.9 %fusion.39 = f32[256,7168]{1,0:T(8,128)} fusion(bf16[256,4096]{1,0:T(8,128)(2,1)S(1)} %multiply_convert_fusion.1, bf16[4096,7168]{1,0:T(8,128)(2,1)} %bitcast.71), kind=kOutput, calls=%fused_computation.110 | convolution fusion | flops 15032385536 | bytes 68157440 | tf_op jit(solution)/shard_map/dot_general | solution.py:24
  611.0 4.6 fusion.1
  626.9 2.8 collective-permute-done.1
  630.4 7.9 collective-permute-done.2
  639.8 2.6 collective-permute-done.4
  643.1 7.1 collective-permute-done.5
  651.0 9.5 %collective-permute-done.6 = bf16[256,512]{1,0:T(8,128)(2,1)S(1)} collective-permute-done((bf16[256,512]{1,0:T(8,128)(2,1)S(1)}, bf16[256,512]{1,0:T(8,128)(2,1)S(1)}, u32[]{:S(2)}, u32[]{:S(2)}) %collective-permute-start.6) | collective-permute-done | bytes 262176 | tf_op jit(solution)/shard_map/ppermute | solution.py:87
  661.2 114.8 %all-gather.5.cloned.1.call-done = bf16[2048,7168]{1,0:T(8,128)(2,1)} async-done(((bf16[256,7168]{1,0:T(8,128)(2,1)}), bf16[2048,7168]{1,0:T(8,128)(2,1)}) %all-gather.5.cloned.1.call-update) | async-done | bytes 29360144 | tf_op jit(solution)/shard_map/all_gather | solution.py:92
  775.9 26.3 %multiply_reduce_fusion = (f32[]{:T(128)}, f32[512,7168]{1,0:T(8,128)}) fusion(bf16[2048,512]{1,0:T(8,128)(2,1)} %constant_dynamic-update-slice_fusion, bf16[2048,7168]{1,0:T(8,128)(2,1)} %all-gather.5.cloned.1.call-done), kind=kOutput, calls=%fused_computation.1 | convolution fusion | flops 15039725568 | bytes 46137348 | tf_op jit(solution)/shard_map/dot_general | solution.py:90
  802.3 39.7 %psum.55 = f32[]{:T(128)} all-reduce(f32[]{:T(128)} %get-tuple-element.33), channel_id=1, replica_groups=mesh['tensor'=4,'dp'=4,'replica'=2] {'tensor','dp','replica'}, use_global_device_ids=true, to_apply=%region_17.18 | all-reduce | flops 1 | bytes 8 | tf_op jit(solution)/shard_map/psum | solution.py:96
  842.7 9.8 %multiply_convert_fusion = bf16[512,7168]{1,0:T(8,128)(2,1)} fusion(f32[512,7168]{1,0:T(8,128)} %get-tuple-element.34, f32[]{:T(128)S(6)} %rsqrt.75), kind=kLoop, calls=%fused_computation | loop fusion | flops 7340032 | bytes 22020100 | tf_op jit(solution)/shard_map/convert_element_type | solution.py:97
  852.5 16.9 %reshape.110 = bf16[512,2,3584]{2,1,0:T(2,128)(2,1)} reshape(bf16[512,7168]{1,0:T(8,128)(2,1)} %multiply_convert_fusion) | data formatting | bytes 14680064 | tf_op jit(solution)/shard_map/reshape | solution.py:98
  (77 shorter events, 38.6 us)
Async XLA Ops:
  7.2 89.3 %all-gather.3.cloned.1.call-start = ((), (), s32[]{:S(2)}) async-start(), calls=%async_computation | async-start | bytes 88080384 | tf_op jit(solution)/shard_map/all_gather | solution.py:41
  7.9 4.6 copy-start.1
  7.9 4.6 copy-start.2
  7.9 214.9 %all-reduce.7.cloned.1.call-start = ((), (), s32[]{:S(2)}) async-start(), calls=%async_computation.1 | async-start | bytes 1048576 | tf_op jit(solution)/shard_map/psum | solution.py:63
  96.4 39.3 %copy-start.4 = (f32[4096]{0:T(1024)S(1)}, f32[4096]{0:T(1024)}, u32[]{:S(2)}) copy-start(f32[4096]{0:T(1024)} %param.9) | copy-start | bytes 49156
  183.2 43.0 %copy-start.6 = (f32[3]{0:T(128)S(1)}, f32[3]{0:T(128)}, u32[]{:S(2)}) copy-start(f32[3]{0:T(128)} %param.13) | copy-start | bytes 40
  183.3 97.6 %all-reduce.9.cloned.1.call-start = ((), (), s32[]{:S(2)}) async-start(), calls=%async_computation.2 | async-start | bytes 1048576 | tf_op jit(solution)/shard_map/psum | solution.py:64
  226.2 143.1 %all-reduce.11.cloned.1.call-start = ((), (), s32[]{:S(2)}) async-start(), calls=%async_computation.3 | async-start | bytes 1048576 | tf_op jit(solution)/shard_map/psum | solution.py:63
  331.5 96.9 %copy-start.3 = (f32[32,4096]{1,0:T(8,128)S(1)}, f32[32,4096]{1,0:T(8,128)}, u32[]{:S(2)}) copy-start(f32[32,4096]{1,0:T(8,128)} %all-reduce.9.cloned.1.call-done) | copy-start | bytes 1572868
  331.6 95.7 %all-reduce.13.cloned.1.call-start = ((), (), s32[]{:S(2)}) async-start(), calls=%async_computation.4 | async-start | bytes 1048576 | tf_op jit(solution)/shard_map/psum | solution.py:64
  372.6 143.8 %all-reduce.15.cloned.1.call-start = ((), (), s32[]{:S(2)}) async-start(), calls=%async_computation.5 | async-start | bytes 1048576 | tf_op jit(solution)/shard_map/psum | solution.py:63
  478.6 95.8 %all-reduce.17.cloned.1.call-start = ((), (), s32[]{:S(2)}) async-start(), calls=%async_computation.6 | async-start | bytes 1048576 | tf_op jit(solution)/shard_map/psum | solution.py:64
  519.7 256.3 %all-gather.5.cloned.1.call-start = ((), (), s32[]{:S(2)}) async-start(), calls=%async_computation.7 | async-start | bytes 33030144 | tf_op jit(solution)/shard_map/all_gather | solution.py:92
  581.1 3.4 copy-start
  619.1 1.3 copy-start.5
  620.4 5.1 collective-permute-start
  620.4 9.3 %collective-permute-start.1 = (bf16[256,512]{1,0:T(8,128)(2,1)}, bf16[256,512]{1,0:T(8,128)(2,1)S(1)}, u32[]{:S(2)}, u32[]{:S(2)}) collective-permute-start(bf16[256,512]{1,0:T(8,128)(2,1)} %get-tuple-element.21), channel_id=1, source_target_pairs={{0,2},{1,3},{2,0},{3,1},{4,6},{5,7},{6,4},{7,5},{8,10},{9,11},{10,... | collective-permute-start | bytes 786440 | tf_op jit(solution)/shard_map/ppermute | solution.py:87
  621.2 17.2 %collective-permute-start.2 = (bf16[256,512]{1,0:T(8,128)(2,1)S(1)}, bf16[256,512]{1,0:T(8,128)(2,1)S(1)}, u32[]{:S(2)}, u32[]{:S(2)}) collective-permute-start(bf16[256,512]{1,0:T(8,128)(2,1)S(1)} %get-tuple-element.20), channel_id=1, source_target_pairs={{0,3},{1,2},{2,1},{3,0},{4,7},{5,6},{6,5},{7,4},{8,11},{9,10},{10,... | collective-permute-start | bytes 786440 | tf_op jit(solution)/shard_map/ppermute | solution.py:87
  622.3 16.9 %collective-permute-start.3 = (bf16[256,512]{1,0:T(8,128)(2,1)S(1)}, bf16[256,512]{1,0:T(8,128)(2,1)S(1)}, u32[]{:S(2)}, u32[]{:S(2)}) collective-permute-start(bf16[256,512]{1,0:T(8,128)(2,1)S(1)} %get-tuple-element.19), channel_id=1, source_target_pairs={{0,4},{1,5},{2,6},{3,7},{4,0},{5,1},{6,2},{7,3},{8,12},{9,13},{10,... | collective-permute-start | bytes 786440 | tf_op jit(solution)/shard_map/ppermute | solution.py:87
  623.0 19.5 %collective-permute-start.4 = (bf16[256,512]{1,0:T(8,128)(2,1)S(1)}, bf16[256,512]{1,0:T(8,128)(2,1)S(1)}, u32[]{:S(2)}, u32[]{:S(2)}) collective-permute-start(bf16[256,512]{1,0:T(8,128)(2,1)S(1)} %get-tuple-element.18), channel_id=1, source_target_pairs={{0,5},{1,4},{2,7},{3,6},{4,1},{5,0},{6,3},{7,2},{8,13},{9,12},{10,... | collective-permute-start | bytes 786440 | tf_op jit(solution)/shard_map/ppermute | solution.py:87
  625.5 24.8 %collective-permute-start.5 = (bf16[256,512]{1,0:T(8,128)(2,1)S(1)}, bf16[256,512]{1,0:T(8,128)(2,1)S(1)}, u32[]{:S(2)}, u32[]{:S(2)}) collective-permute-start(bf16[256,512]{1,0:T(8,128)(2,1)S(1)} %get-tuple-element.17), channel_id=1, source_target_pairs={{0,6},{1,7},{2,4},{3,5},{4,2},{5,3},{6,0},{7,1},{8,14},{9,15},{10,... | collective-permute-start | bytes 786440 | tf_op jit(solution)/shard_map/ppermute | solution.py:87
  629.7 30.8 %collective-permute-start.6 = (bf16[256,512]{1,0:T(8,128)(2,1)S(1)}, bf16[256,512]{1,0:T(8,128)(2,1)S(1)}, u32[]{:S(2)}, u32[]{:S(2)}) collective-permute-start(bf16[256,512]{1,0:T(8,128)(2,1)S(1)} %get-tuple-element.16), channel_id=1, source_target_pairs={{0,7},{1,6},{2,5},{3,4},{4,3},{5,2},{6,1},{7,0},{8,15},{9,14},{10,... | collective-permute-start | bytes 786440 | tf_op jit(solution)/shard_map/ppermute | solution.py:87
Sparse Core Ops, SparseCore 0:
  9.5 86.8 all-gather.2
  183.4 39.4 all-reduce.6
  226.3 54.5 all-reduce.8
  331.7 37.5 all-reduce.10
  372.7 54.5 all-reduce.12
  478.7 37.5 all-reduce.14
  519.8 54.5 all-reduce.16
  618.0 157.9 all-gather.4
